TPU v7x, 256 devices: a whole 4x4x8 slice. The times are simulated.
256 devices in a mesh: row: 32 (over x, z), col: 8 (over y, core).
Axes of the slice: x: 4, y: 4, z: 8, core: 2. Of those that a mesh axis runs over, the one named last changes fastest.
Arguments:
- tensor: bfloat16 [64, 2048, 2048], P(None, 'row', 'col'), may hold values from -6 to 6
- pattern: int32 [32, 32], P('col', 'row'), may hold values 0 or 1
- coef: bfloat16 [2048, 2048], P('row', 'col'), may hold values from -0.1875 to 0.1875
Outputs:
- contracted: bfloat16 [64, 2048, 2048], P(None, 'row', 'col')
All inputs are finite; a program needn't handle non-finite values. No bound on the sum of `pattern` on one device may be relied on, other than what follows from the above.
Results may differ from a plain program's by a relative error of at most 0.001.
Values may be sent and summed in bfloat16 or wider, within the bound.
A program may use at most 64 MiB of HBM per device.

v0:
```python
import jax
import jax.numpy as jnp
from jax import lax
from jax.sharding import PartitionSpec as P


def per_device(tensor, pattern, coef):
    mu_all, nu_loc, aux_loc = tensor.shape
    atoms_aux, atoms_nu = pattern.shape
    blk = aux_loc // atoms_aux
    keep = jnp.transpose(pattern).astype(jnp.bfloat16)[None, :, None, :, None]
    masked = (tensor.reshape(mu_all, atoms_nu, blk, atoms_aux, blk) * keep).reshape(
        mu_all, nu_loc, aux_loc
    )
    matrix = lax.all_to_all(masked, "row", split_axis=0, concat_axis=1, tiled=True)
    form = "mna,no->moa"
    panel = lax.all_gather(coef, "col", axis=1, tiled=True)
    whole = lax.all_gather(panel, "row", axis=0, tiled=True)
    product = jnp.einsum(form, matrix, whole, preferred_element_type=jnp.float32)
    result = product.astype(jnp.bfloat16)
    return lax.all_to_all(result, "row", split_axis=1, concat_axis=0, tiled=True)


def solution(mesh):
    return jax.shard_map(
        per_device,
        mesh=mesh,
        in_specs=(P(None, "row", "col"), P("col", "row"), P("row", "col")),
        out_specs=P(None, "row", "col"),
        check_vma=False,
    )
```

profile of v0, /device:TPU:8, one launch (start us, length us, event | category | flops | bytes accessed | tf_op | source)
XLA Modules:
  0.0 217.4 jit_solution(12455503580650013508)
XLA Ops:
  6.5 0.0 all-gather.2.cloned.1.call-start
  6.5 14.4 %all_gather.6 = bf16[64,2048]{1,0:T(8,128)(2,1)} all-gather(bf16[64,256]{1,0:T(8,128)(2,1)} %param.5), channel_id=1, replica_groups=mesh['row'=32,'col'=8] {'col'}, dimensions={1}, use_global_device_ids=true | all-gather | bytes 294912 | tf_op jit(solution)/shard_map/all_gather | solution.py:17
  21.0 0.0 all-gather.2.cloned.1.call-update
  21.0 0.7 convert_bitcast_fusion
  21.7 0.1 mul.15
  21.7 0.1 mul.16
  21.8 1.7 broadcast_multiply_fusion
  23.5 72.5 %all_to_all.36 = bf16[64,64,256]{2,1,0:T(8,128)(2,1)S(1)} all-to-all(bf16[64,64,256]{2,1,0:T(8,128)(2,1)S(1)} %broadcast_multiply_fusion), channel_id=1, replica_groups=mesh['row'=32,'col'=8] {'row'}, dimensions={0} | all-to-all | bytes 4194304 | tf_op jit(solution)/shard_map/all_to_all | solution.py:15
  96.1 0.1 copy.12
  96.2 41.9 %all-gather.2.cloned.1.call-done = bf16[2048,2048]{1,0:T(8,128)(2,1)} async-done(((bf16[64,2048]{1,0:T(8,128)(2,1)}), bf16[2048,2048]{1,0:T(8,128)(2,1)}) %all-gather.2.cloned.1.call-update) | async-done | bytes 8388624 | tf_op jit(solution)/shard_map/all_gather | solution.py:18
  138.1 9.1 %fusion.5 = bf16[2,2048,256]{1,2,0:T(8,128)(2,1)} fusion(bf16[2,2048,256]{2,1,0:T(8,128)(2,1)S(1)} %bitcast.22, bf16[2048,2048]{1,0:T(8,128)(2,1)} %all-gather.2.cloned.1.call-done), kind=kOutput, calls=%fused_computation.3 | convolution fusion | flops 4296015872 | bytes 12582912 | tf_op jit(solution)/shard_map/mna,no->moa/dot_general | solution.py:19
  147.2 4.8 %copy.14 = bf16[2,2048,256]{2,0,1:T(2,128)(2,1)S(1)} copy(bf16[2,2048,256]{1,2,0:T(8,128)(2,1)} %fusion.5) | data formatting | bytes 4194304 | tf_op jit(solution)/shard_map/convert_element_type | solution.py:20
  152.0 56.7 %all_to_all.37 = bf16[2,2048,256]{2,0,1:T(2,128)(2,1)S(1)} all-to-all(bf16[2,2048,256]{2,0,1:T(2,128)(2,1)S(1)} %copy.14), channel_id=1, replica_groups=mesh['row'=32,'col'=8] {'row'}, dimensions={1} | all-to-all | bytes 4194304 | tf_op jit(solution)/shard_map/all_to_all | solution.py:21
  208.8 0.3 copy.15
  209.1 1.5 copy.16
Async XLA Ops:
  6.5 131.6 %all-gather.2.cloned.1.call-start = ((), (), s32[]{:S(2)}) async-start(), calls=%async_computation.2 | async-start | bytes 8650752 | tf_op jit(solution)/shard_map/all_gather | solution.py:18
Sparse Core Ops, SparseCore 0:
  21.1 116.9 all-gather.1
where the time goes:
time: 218 us; the launch traced here: 217 us
  blocking collectives  144 us (66%)
  waiting for transfers between devices  41.9 us (19%)
  between operations  13.4 us (6%)
  matrix products  9.1 us (4%)
  local copies, waits for them, and re-layouts  6.85 us (3%)
  other arithmetic  2.39 us (1%)
    all_to_all x1, blocking collectives, per_device(): lax.all_to_all(masked, 'row', split_axis=0, concat_axis=1, tiled=True)  72.5 us
    all_to_all x1, blocking collectives, per_device(): lax.all_to_all(result, 'row', split_axis=1, concat_axis=0, tiled=True)  56.7 us
    all_gather x1, waiting for transfers between devices, per_device(): whole = lax.all_gather(panel, 'row', axis=0, tiled=True)  41.9 us
    all_gather x1, blocking collectives, per_device(): panel = lax.all_gather(coef, 'col', axis=1, tiled=True)  14.4 us
    dot_general x1, matrix products, per_device(): jnp.einsum(form, matrix, whole, preferred_element_type=jnp.float32)  9.1 us
    convert_element_type x1, local copies, waits for them, and re-layouts, per_device(): result = product.astype(jnp.bfloat16)  4.82 us
  transfers between devices with their start and end apart: 1, of which 1 were waited for; matrix products, arithmetic and copies ran while one was open for 1% of the time, Pallas kernels for 0%

commit v1 on v0

--- a/solution.py
+++ b/solution.py
@@ -2,6 +2,22 @@
 import jax.numpy as jnp
 from jax import lax
 from jax.sharding import PartitionSpec as P
+
+
+def collect(x, axis, dim):
+    ways, here, step = (lax.axis_size(axis), lax.axis_index(axis), x.shape[dim])
+    lengths = [n * ways if d == dim else n for d, n in enumerate(x.shape)]
+    full = lax.dynamic_update_slice_in_dim(jnp.zeros(lengths, x.dtype), x, here * step, axis=dim)
+    going_up = going_down = x
+    for far in range(1, ways // 2 + 1):
+        going_up = lax.ppermute(going_up, axis, [(d, (d + 1) % ways) for d in range(ways)])
+        full = lax.dynamic_update_slice_in_dim(full, going_up, (here - far) % ways * step, axis=dim)
+        if 2 * far < ways:
+            going_down = lax.ppermute(going_down, axis, [(d, (d - 1) % ways) for d in range(ways)])
+            full = lax.dynamic_update_slice_in_dim(
+                full, going_down, (here + far) % ways * step, axis=dim
+            )
+    return full
 
 
 def per_device(tensor, pattern, coef):
@@ -14,7 +30,7 @@
     )
     matrix = lax.all_to_all(masked, "row", split_axis=0, concat_axis=1, tiled=True)
     form = "mna,no->moa"
-    panel = lax.all_gather(coef, "col", axis=1, tiled=True)
+    panel = collect(coef, "col", 1)
     whole = lax.all_gather(panel, "row", axis=0, tiled=True)
     product = jnp.einsum(form, matrix, whole, preferred_element_type=jnp.float32)
     result = product.astype(jnp.bfloat16)

time: 218 us -> 228 us (1.046)
  blocking collectives: 144 us -> 128 us
  waiting for transfers between devices: 41.9 us -> 53.9 us
  local copies, waits for them, and re-layouts: 6.85 us -> 16.4 us
  starting transfers between devices: 0.01 us -> 5.14 us
    all_gather x1 -> x0, blocking collectives: 14.4 us -> none  [per_device(): panel = lax.all_gather(coef, 'col', axis=1, tiled=True)]
    convert_element_type x1, local copies, waits for them, and re-layouts: 4.82 us -> 12.8 us  [per_device(): result = product.astype(jnp.bfloat16)]
    ppermute x0 -> x7, waiting for transfers between devices: none -> 7.92 us  [the longest x4 7.8 us: collect(): lax.ppermute(going_up, axis, [(d, (d + 1) % ways) for d in range(ways)])]
    ppermute x0 -> x7, starting transfers between devices: none -> 5.14 us  [the longest x3 5.12 us: collect(): lax.ppermute(going_down, axis, [(d, (d - 1) % ways) for d in range(ways)])]
    all_gather x1, waiting for transfers between devices: 41.9 us -> 46 us  [per_device(): whole = lax.all_gather(panel, 'row', axis=0, tiled=True)]
  transfers between devices with their start and end apart: 1 -> 8, of which waited for: 1 -> 6; matrix products, arithmetic and copies ran while one was open for 1% -> 2% of each run, Pallas kernels for 0% -> 0%
where the time goes in v1:
time: 228 us
  blocking collectives  128 us (56%)
  waiting for transfers between devices  53.9 us (24%)
  local copies, waits for them, and re-layouts  16.4 us (7%)
  between operations  13.5 us (6%)
  matrix products  8.48 us (4%)
  starting transfers between devices  5.14 us (2%)
  other arithmetic  2.39 us (1%)
    all_to_all x1, blocking collectives, per_device(): lax.all_to_all(masked, 'row', split_axis=0, concat_axis=1, tiled=True)  71.4 us
    all_to_all x1, blocking collectives, per_device(): lax.all_to_all(result, 'row', split_axis=1, concat_axis=0, tiled=True)  56.3 us
    all_gather x1, waiting for transfers between devices, per_device(): whole = lax.all_gather(panel, 'row', axis=0, tiled=True)  46 us
    convert_element_type x1, local copies, waits for them, and re-layouts, per_device(): result = product.astype(jnp.bfloat16)  12.8 us
    dot_general x1, matrix products, per_device(): jnp.einsum(form, matrix, whole, preferred_element_type=jnp.float32)  8.48 us
    ppermute x4, waiting for transfers between devices, collect(): lax.ppermute(going_up, axis, [(d, (d + 1) % ways) for d in range(ways)])  7.8 us
    ppermute x3, starting transfers between devices, collect(): lax.ppermute(going_down, axis, [(d, (d - 1) % ways) for d in range(ways)])  5.12 us
  transfers between devices with their start and end apart: 8, of which 6 were waited for; matrix products, arithmetic and copies ran while one was open for 2% of the time, Pallas kernels for 0%

profile of v1, /device:TPU:8, one launch (start us, length us, event | category | flops | bytes accessed | tf_op | source)
XLA Modules:
  0.0 227.5 jit_solution(15837384356146931166)
XLA Ops:
  6.5 0.0 all-gather.2.cloned.1.call-start
  6.5 0.0 collective-permute-start
  6.5 1.7 collective-permute-start.1
  8.3 0.8 constant_dynamic-update-slice_fusion.7
  9.1 1.0 collective-permute-done
  10.1 0.0 collective-permute-start.2
  10.1 0.1 collective-permute-done.1
  10.2 1.6 collective-permute-start.3
  11.9 1.6 collective-permute-done.2
  13.4 0.0 collective-permute-start.4
  13.4 0.0 collective-permute-done.3
  13.4 1.7 collective-permute-start.5
  15.2 1.6 collective-permute-done.4
  16.8 0.0 collective-permute-start.6
  16.8 0.0 collective-permute-done.5
  16.8 3.6 %collective-permute-done.6 = bf16[64,256]{1,0:T(8,128)(2,1)S(1)} collective-permute-done((bf16[64,256]{1,0:T(8,128)(2,1)S(1)}, bf16[64,256]{1,0:T(8,128)(2,1)S(1)}, u32[]{:S(2)}, u32[]{:S(2)}) %collective-permute-start.6) | collective-permute-done | bytes 32800 | tf_op jit(solution)/shard_map/ppermute | solution.py:13
  20.5 0.0 copy-start
  20.5 0.7 copy-done
  21.2 0.0 all-gather.2.cloned.1.call-update
  21.2 0.7 convert_bitcast_fusion
  21.8 0.1 mul.47
  21.9 0.1 mul.48
  22.0 1.7 broadcast_multiply_fusion
  23.7 71.4 %all_to_all.36 = bf16[64,64,256]{2,1,0:T(8,128)(2,1)S(1)} all-to-all(bf16[64,64,256]{2,1,0:T(8,128)(2,1)S(1)} %broadcast_multiply_fusion), channel_id=1, replica_groups=mesh['row'=32,'col'=8] {'row'}, dimensions={0} | all-to-all | bytes 4194304 | tf_op jit(solution)/shard_map/all_to_all | solution.py:31
  95.2 0.1 copy.6
  95.3 46.0 %all-gather.2.cloned.1.call-done = bf16[2048,2048]{1,0:T(8,128)(2,1)} async-done(((bf16[64,2048]{1,0:T(8,128)(2,1)}), bf16[2048,2048]{1,0:T(8,128)(2,1)}) %all-gather.2.cloned.1.call-update) | async-done | bytes 8388624 | tf_op jit(solution)/shard_map/all_gather | solution.py:34
  141.3 8.5 %fusion.5 = bf16[2,2048,256]{2,1,0:T(8,128)(2,1)S(1)} fusion(bf16[2,2048,256]{2,1,0:T(8,128)(2,1)S(1)} %bitcast.22, bf16[2048,2048]{1,0:T(8,128)(2,1)} %all-gather.2.cloned.1.call-done), kind=kOutput, calls=%fused_computation.3 | convolution fusion | flops 4296015872 | bytes 12582912 | tf_op jit(solution)/shard_map/mna,no->moa/dot_general | solution.py:35
  149.8 12.8 %copy.7 = bf16[2,2048,256]{2,0,1:T(2,128)(2,1)S(1)} copy(bf16[2,2048,256]{2,1,0:T(8,128)(2,1)S(1)} %fusion.5) | data formatting | bytes 4194304 | tf_op jit(solution)/shard_map/convert_element_type | solution.py:36
  162.6 56.3 %all_to_all.37 = bf16[2,2048,256]{2,0,1:T(2,128)(2,1)S(1)} all-to-all(bf16[2,2048,256]{2,0,1:T(2,128)(2,1)S(1)} %copy.7), channel_id=1, replica_groups=mesh['row'=32,'col'=8] {'row'}, dimensions={1} | all-to-all | bytes 4194304 | tf_op jit(solution)/shard_map/all_to_all | solution.py:37
  218.9 1.8 copy.8
  (8 shorter events, 0.1 us)
Async XLA Ops:
  6.5 134.8 %all-gather.2.cloned.1.call-start = ((), (), s32[]{:S(2)}) async-start(), calls=%async_computation.2 | async-start | bytes 8650752 | tf_op jit(solution)/shard_map/all_gather | solution.py:34
  6.5 3.6 %collective-permute-start = (bf16[64,256]{1,0:T(8,128)(2,1)}, bf16[64,256]{1,0:T(8,128)(2,1)S(1)}, u32[]{:S(2)}, u32[]{:S(2)}) collective-permute-start(bf16[64,256]{1,0:T(8,128)(2,1)} %param.5), channel_id=1, source_target_pairs={{0,1},{1,2},{2,3},{3,4},{4,5},{5,6},{6,7},{7,0},{8,9},{9,10},{10,1... | collective-permute-start | bytes 98312 | tf_op jit(solution)/shard_map/ppermute | solution.py:13
  6.5 3.7 %collective-permute-start.1 = (bf16[64,256]{1,0:T(8,128)(2,1)}, bf16[64,256]{1,0:T(8,128)(2,1)S(1)}, u32[]{:S(2)}, u32[]{:S(2)}) collective-permute-start(bf16[64,256]{1,0:T(8,128)(2,1)} %param.5), channel_id=1, source_target_pairs={{0,7},{1,0},{2,1},{3,2},{4,3},{5,4},{6,5},{7,6},{8,15},{9,8},{10,9... | collective-permute-start | bytes 98312 | tf_op jit(solution)/shard_map/ppermute | solution.py:16
  10.1 3.3 %collective-permute-start.2 = (bf16[64,256]{1,0:T(8,128)(2,1)S(1)}, bf16[64,256]{1,0:T(8,128)(2,1)S(1)}, u32[]{:S(2)}, u32[]{:S(2)}) collective-permute-start(bf16[64,256]{1,0:T(8,128)(2,1)S(1)} %collective-permute-done), channel_id=1, source_target_pairs={{0,1},{1,2},{2,3},{3,4},{4,5},{5,6},{6,7},{7,0},{8,9},{9,10},{10,1... | collective-permute-start | bytes 98312 | tf_op jit(solution)/shard_map/ppermute | solution.py:13
  10.2 3.2 %collective-permute-start.3 = (bf16[64,256]{1,0:T(8,128)(2,1)S(1)}, bf16[64,256]{1,0:T(8,128)(2,1)S(1)}, u32[]{:S(2)}, u32[]{:S(2)}) collective-permute-start(bf16[64,256]{1,0:T(8,128)(2,1)S(1)} %collective-permute-done.1), channel_id=1, source_target_pairs={{0,7},{1,0},{2,1},{3,2},{4,3},{5,4},{6,5},{7,6},{8,15},{9,8},{10,9... | collective-permute-start | bytes 98312 | tf_op jit(solution)/shard_map/ppermute | solution.py:16
  13.4 3.3 %collective-permute-start.4 = (bf16[64,256]{1,0:T(8,128)(2,1)S(1)}, bf16[64,256]{1,0:T(8,128)(2,1)S(1)}, u32[]{:S(2)}, u32[]{:S(2)}) collective-permute-start(bf16[64,256]{1,0:T(8,128)(2,1)S(1)} %collective-permute-done.2), channel_id=1, source_target_pairs={{0,1},{1,2},{2,3},{3,4},{4,5},{5,6},{6,7},{7,0},{8,9},{9,10},{10,1... | collective-permute-start | bytes 98312 | tf_op jit(solution)/shard_map/ppermute | solution.py:13
  13.4 3.3 %collective-permute-start.5 = (bf16[64,256]{1,0:T(8,128)(2,1)S(1)}, bf16[64,256]{1,0:T(8,128)(2,1)S(1)}, u32[]{:S(2)}, u32[]{:S(2)}) collective-permute-start(bf16[64,256]{1,0:T(8,128)(2,1)S(1)} %collective-permute-done.3), channel_id=1, source_target_pairs={{0,7},{1,0},{2,1},{3,2},{4,3},{5,4},{6,5},{7,6},{8,15},{9,8},{10,9... | collective-permute-start | bytes 98312 | tf_op jit(solution)/shard_map/ppermute | solution.py:16
  16.8 3.7 %collective-permute-start.6 = (bf16[64,256]{1,0:T(8,128)(2,1)S(1)}, bf16[64,256]{1,0:T(8,128)(2,1)S(1)}, u32[]{:S(2)}, u32[]{:S(2)}) collective-permute-start(bf16[64,256]{1,0:T(8,128)(2,1)S(1)} %collective-permute-done.4), channel_id=1, source_target_pairs={{0,1},{1,2},{2,3},{3,4},{4,5},{5,6},{6,7},{7,0},{8,9},{9,10},{10,1... | collective-permute-start | bytes 98312 | tf_op jit(solution)/shard_map/ppermute | solution.py:13
  20.5 0.7 copy-start
Sparse Core Ops, SparseCore 0:
  21.3 119.9 all-gather.1
